TPU v7x, 32 devices: a whole 2x2x4 slice. The times are simulated.
32 devices in a mesh: dp: 8 (over z, x), zero: 4 (over y, core).
Axes of the slice: x: 2, y: 2, z: 4, core: 2. Of those that a mesh axis runs over, the one named last changes fastest.
Arguments:
- tokens: bfloat16 [64, 1024, 768], P('zero', 'dp'), may hold values from -6 to 6
- loss_sensitivity: bfloat16 [32, 1024, 768], P(('dp', 'zero')), may hold values from -6 to 6
- lengths: int32 [64], replicated, may hold values from 0 to 1024, as said below
- holder_sequence_list: int32 [64], replicated, may hold values from 0 to 63, as said below
- master: float32 [3768320], P('zero')
- moment_one: float32 [3768320], P('zero'), may hold values from -18 to 18
- moment_two: float32 [3768320], P('zero'), may hold values from 1 to 1000
- adam_rates: float32 [2], replicated, may hold values from 0.05 to 0.2
- iteration_tally: int32 [1], replicated, may hold values from 1 to 8
Outputs:
- tokens_out: bfloat16 [64, 1024, 768], P('zero', 'dp')
- grad_tokens: bfloat16 [64, 1024, 768], P('zero', 'dp')
- new_master: float32 [3768320], replicated
- grads: float32 [3768320], P('zero')
- moment_one_out: float32 [3768320], P('zero')
- moment_two_out: float32 [3768320], P('zero')
Inputs may be any that keep to these rules, and one draw needn't show every extreme that they name: A permutation of the sequences. Slot i lies on the device whose index along dp+zero is i // 2, and holder_sequence_list[i] is one of the 64 / 4 sequences of that device's zero index (sequences z * 64 / 4 onward for zero index z). The two sequences of slots 2j and 2j + 1 have lengths summing to exactly 1024; in some pack one of them has 1024 tokens and the other none.
All inputs are finite; a program needn't handle non-finite values.
Results may differ from a plain program's by a relative error of at most 0.002.
The roundings to bfloat16 on the way count: a program that leaves them out, or rounds other values in their place, can miss the bound.
Values may be sent and summed in bfloat16 or wider, within the bound.
No kernel may reach another device: no remote copies, remote signals or barrier semaphores. Data moves between devices by JAX's collectives and lax.ppermute only.
A program may use at most 256 MiB of HBM per device.

v0:
```python
from functools import partial
import jax
import jax.numpy as jnp
from jax import lax
from jax.sharding import PartitionSpec as P

D = 768
HEADS = 24
HEADDIM = 64
STATE = 128
CONV = 4
SPAN = 256
INNER = 1536
XBC = 1792
PROJ = 3352
EXACT_MATMUL = lax.Precision.HIGHEST
EPS_NORM = 1e-05
BETA_ONE = 0.9
BETA_TWO = 0.95
EPS_ADAM = 1e-08


def padded_slot(amount):
    return (amount + 127) // 128 * 128


def unpack(linear_coefficient_list):
    piece_sizes = [D, D * PROJ, CONV * XBC, XBC, HEADS, HEADS, HEADS, INNER, INNER * D]
    pieces = []
    offset = 0
    for amount in piece_sizes:
        pieces.append(linear_coefficient_list[offset : offset + amount])
        offset = offset + padded_slot(amount)
    (
        norm_gain,
        input_weight_t,
        conv_w,
        conv_b,
        dt_bias,
        a_log,
        d_skip,
        gated_gain,
        emitting_matrix,
    ) = pieces
    return (
        norm_gain,
        input_weight_t.reshape(PROJ, D),
        conv_w.reshape(CONV, XBC),
        conv_b,
        dt_bias,
        a_log,
        d_skip,
        gated_gain,
        emitting_matrix.reshape(INNER, D),
    )


def pre_norm(values, gain):
    return values * lax.rsqrt(jnp.mean(values * values, axis=-1, keepdims=True) + EPS_NORM) * gain


def causal_conv(conv_in, conv_w, conv_b, segment):
    seq_len = conv_in.shape[1]
    padded = jnp.pad(conv_in, ((0, 0), (CONV - 1, 0), (0, 0)))
    seg_padded = jnp.pad(segment, ((0, 0), (CONV - 1, 0)), constant_values=-1.0)
    summed = conv_b + jnp.zeros_like(conv_in)
    for offset in range(CONV):
        same_seg = (seg_padded[:, offset : offset + seq_len] == segment).astype(jnp.float32)[
            ..., None
        ]
        summed = summed + conv_w[offset] * (padded[:, offset : offset + seq_len] * same_seg)
    return summed


def span_scan(x_heads, dt_pos, decay_rate, b_rows, c_rows, segment):
    batch_size, seq_len, head_count, head_width = x_heads.shape
    block_count = seq_len // SPAN

    def split_blocks(values):
        shaped = values.reshape((batch_size, block_count, SPAN) + values.shape[2:])
        return jnp.moveaxis(shaped, 1, 0)

    causal = jnp.arange(SPAN)[:, None] >= jnp.arange(SPAN)[None, :]

    def advance(carried_pair, block_in):
        carried, last_seg = carried_pair
        x_blk, dt_blk, b_blk, c_blk, membership_tile = block_in
        dt_cols = jnp.swapaxes(dt_blk, 1, 2)
        cum_blk = jnp.cumsum(dt_cols * decay_rate[None, :, None], axis=2)
        differ = cum_blk[:, :, :, None] - cum_blk[:, :, None, :]
        same_seg = membership_tile[:, :, None] == membership_tile[:, None, :]
        allowed = jnp.logical_and(causal[None], same_seg)[:, None]
        weights_in = jnp.exp(jnp.where(allowed, differ, -jnp.inf))
        gram_blk = jnp.einsum("stn,srn->str", c_blk, b_blk, precision=EXACT_MATMUL)
        mixing = gram_blk[:, None] * weights_in * dt_cols[:, :, None, :]
        inside = jnp.einsum("shtr,srhp->sthp", mixing, x_blk, precision=EXACT_MATMUL)
        from_state = jnp.einsum("stn,shpn->sthp", c_blk, carried, precision=EXACT_MATMUL)
        from_state = from_state * jnp.swapaxes(jnp.exp(cum_blk), 1, 2)[..., None]
        keep_state = (membership_tile == last_seg[:, None]).astype(jnp.float32)
        from_state = from_state * keep_state[:, :, None, None]
        cum_end = cum_blk[:, :, -1]
        end_seg = membership_tile[:, -1]
        in_last = (membership_tile == end_seg[:, None]).astype(jnp.float32)
        carry_weight = jnp.exp(cum_end[:, :, None] - cum_blk) * dt_cols * in_last[:, None, :]
        added_state = jnp.einsum(
            "srn,shr,srhp->shpn", b_blk, carry_weight, x_blk, precision=EXACT_MATMUL
        )
        carry_scale = jnp.exp(cum_end) * (end_seg == last_seg).astype(jnp.float32)[:, None]
        carried = carried * carry_scale[:, :, None, None] + added_state
        return ((carried, end_seg), inside + from_state)

    initial = (
        jnp.zeros((batch_size, head_count, head_width, b_rows.shape[-1]), jnp.float32),
        jnp.zeros((batch_size,), jnp.float32),
    )
    final_pair, outputs = lax.scan(
        jax.checkpoint(advance),
        initial,
        (
            split_blocks(x_heads),
            split_blocks(dt_pos),
            split_blocks(b_rows),
            split_blocks(c_rows),
            split_blocks(segment),
        ),
    )
    return jnp.moveaxis(outputs, 0, 1).reshape(batch_size, seq_len, head_count, head_width)


def mixer_branch(input_projection, conv_w, conv_b, dt_bias, a_log, d_skip, gated_gain, segment):
    batch_size, seq_len = (input_projection.shape[0], input_projection.shape[1])
    gate_z = input_projection[..., :INNER]
    conv_in = input_projection[..., INNER : INNER + XBC]
    dt_raw = input_projection[..., INNER + XBC :]
    conv_out = jax.nn.silu(causal_conv(conv_in, conv_w, conv_b, segment))
    x_heads = conv_out[..., :INNER].reshape(batch_size, seq_len, HEADS, HEADDIM)
    b_rows = conv_out[..., INNER : INNER + STATE]
    c_rows = conv_out[..., INNER + STATE :]
    dt_pos = jax.nn.softplus(dt_raw + dt_bias)
    decay_rate = -jnp.exp(a_log)
    scanned = (
        span_scan(x_heads, dt_pos, decay_rate, b_rows, c_rows, segment) + d_skip[:, None] * x_heads
    )
    gated_out = scanned.reshape(batch_size, seq_len, INNER) * jax.nn.silu(gate_z)
    return (
        gated_out
        * lax.rsqrt(jnp.mean(gated_out * gated_out, axis=-1, keepdims=True) + EPS_NORM)
        * gated_gain
    )


def adam_update(weights, first_moment, second_moment, gradient, adam_rates, iteration_tally):
    steps_f = iteration_tally[0].astype(jnp.float32)
    first_next = BETA_ONE * first_moment + (1.0 - BETA_ONE) * gradient
    second_next = BETA_TWO * second_moment + (1.0 - BETA_TWO) * gradient * gradient
    first_hat = first_next / (1.0 - jnp.power(BETA_ONE, steps_f))
    second_hat = second_next / (1.0 - jnp.power(BETA_TWO, steps_f))
    updated = weights - adam_rates[0] * (
        first_hat / (jnp.sqrt(second_hat) + EPS_ADAM) + adam_rates[1] * weights
    )
    return (updated, first_next, second_next)


def on_device(
    tokens,
    loss_sensitivity,
    lengths,
    holder_sequence_list,
    master,
    moment_one,
    moment_two,
    adam_rates,
    iteration_tally,
):
    group_devices = lax.axis_size("zero")
    data_devices = lax.axis_size("dp")
    zero_index = lax.axis_index("zero")
    dp_index = lax.axis_index("dp")
    pack_count = loss_sensitivity.shape[0]
    slot_count = 2 * pack_count
    seq_len = loss_sensitivity.shape[1]
    model_width = loss_sensitivity.shape[2]
    group_seqs = tokens.shape[0]
    full_weights = lax.all_gather(master.astype(jnp.bfloat16), "zero", axis=0, tiled=True)
    (
        norm_gain,
        input_weight_t,
        conv_w,
        conv_b,
        dt_bias,
        a_log,
        d_skip,
        gated_gain,
        emitting_matrix,
    ) = unpack(full_weights)
    small_f = [
        piece.astype(jnp.float32) for piece in (conv_w, conv_b, dt_bias, a_log, d_skip, gated_gain)
    ]
    norm_gain_f = norm_gain.astype(jnp.float32)
    arranged_order = holder_sequence_list.reshape(data_devices, group_devices, slot_count)
    group_order = lax.dynamic_index_in_dim(arranged_order, zero_index, 1, keepdims=False).reshape(
        -1
    )
    local_ids = group_order - zero_index * group_seqs
    dealt_rows = jnp.take(tokens, local_ids, axis=0)
    local_tok = lax.all_to_all(dealt_rows, "dp", split_axis=0, concat_axis=1, tiled=True)
    my_seqs = lax.dynamic_slice_in_dim(group_order, dp_index * slot_count, slot_count)
    my_lengths = jnp.take(lengths, my_seqs)
    bounds = my_lengths.reshape(pack_count, 2)[:, 0]
    positions = jnp.arange(seq_len, dtype=jnp.int32)
    later_part = positions[None, :] >= bounds[:, None]
    pack_ids = jnp.arange(pack_count, dtype=jnp.int32)[:, None]
    source = jnp.where(
        later_part,
        (2 * pack_ids + 1) * seq_len + positions[None, :] - bounds[:, None],
        2 * pack_ids * seq_len + positions[None, :],
    )
    segment = later_part.astype(jnp.float32)
    slot_rows = local_tok.reshape(slot_count * seq_len, model_width)
    packed_tok = jnp.take(slot_rows, source.reshape(-1), axis=0).reshape(
        pack_count, seq_len, model_width
    )
    place_numbering = jnp.arange(slot_count, dtype=jnp.int32)
    shift_by = jnp.where(place_numbering % 2 == 1, jnp.repeat(bounds, 2), 0)
    within = positions[None, :] + shift_by[:, None]
    unpack_rows = (place_numbering // 2)[:, None] * seq_len + jnp.minimum(within, seq_len - 1)
    slot_live = (positions[None, :] < my_lengths[:, None]).astype(jnp.float32)[..., None]

    def to_slots(values):
        flat_rows = values.reshape(pack_count * seq_len, values.shape[2])
        picked = jnp.take(flat_rows, unpack_rows.reshape(-1), axis=0)
        return picked.reshape(slot_count, seq_len, values.shape[2]) * slot_live

    tokens_f = packed_tok.astype(jnp.float32)
    normalized, norm_pull = jax.vjp(pre_norm, tokens_f, norm_gain_f)
    normalized_rows = normalized.astype(jnp.bfloat16)
    input_projection = jnp.einsum(
        "mgv,bv->mgb", normalized_rows, input_weight_t, preferred_element_type=jnp.float32
    )
    mixer_output, mix_pull = jax.vjp(
        partial(mixer_branch, segment=segment), input_projection, *small_f
    )
    mixer_output_rows = mixer_output.astype(jnp.bfloat16)
    mixer_path = jnp.einsum(
        "ocr,rb->ocb", mixer_output_rows, emitting_matrix, preferred_element_type=jnp.float32
    )
    result = (local_tok.astype(jnp.float32) + to_slots(mixer_path)).astype(jnp.bfloat16)
    cot_f = loss_sensitivity.astype(jnp.float32)
    grad_out_weight = jnp.einsum(
        "uir,uin->rn", mixer_output_rows, loss_sensitivity, preferred_element_type=jnp.float32
    )
    grad_mixed = jnp.einsum(
        "nsa,wa->nsw", loss_sensitivity, emitting_matrix, preferred_element_type=jnp.float32
    )
    grad_proj, grad_conv_w, grad_conv_b, grad_dt_bias, grad_a_log, grad_d_skip, grad_gated = (
        mix_pull(grad_mixed)
    )
    grad_projection_rows = grad_proj.astype(jnp.bfloat16)
    grad_in_weight_t = jnp.einsum(
        "pvr,pvy->ry", grad_projection_rows, normalized_rows, preferred_element_type=jnp.float32
    )
    grad_normed = jnp.einsum(
        "ept,tb->epb", grad_projection_rows, input_weight_t, preferred_element_type=jnp.float32
    )
    grad_tok, grad_norm_gain = norm_pull(grad_normed)
    grad_input = to_slots(cot_f + grad_tok).astype(jnp.bfloat16)
    back_out, back_grad = (
        lax.all_to_all(result, "dp", split_axis=1, concat_axis=0, tiled=True),
        lax.all_to_all(grad_input, "dp", split_axis=1, concat_axis=0, tiled=True),
    )
    restore = jnp.zeros_like(local_ids).at[local_ids].set(jnp.arange(group_seqs, dtype=jnp.int32))
    tokens_out = jnp.take(back_out, restore, axis=0)
    grad_tokens = jnp.take(back_grad, restore, axis=0)
    vector_len = master.shape[0] * group_devices
    used = [
        grad_norm_gain,
        grad_in_weight_t.reshape(-1),
        grad_conv_w.reshape(-1),
        grad_conv_b,
        grad_dt_bias,
        grad_a_log,
        grad_d_skip,
        grad_gated,
        grad_out_weight.reshape(-1),
    ]
    laid = [jnp.pad(piece, (0, padded_slot(piece.shape[0]) - piece.shape[0])) for piece in used]
    used_len = sum((piece.shape[0] for piece in laid))
    flat_grad = jnp.concatenate(laid + [jnp.zeros((vector_len - used_len,), jnp.float32)])
    grad_shard = lax.psum_scatter(flat_grad, "zero", scatter_dimension=0, tiled=True)
    grad_shard = lax.psum(grad_shard, "dp")
    new_shard, first_next, second_next = adam_update(
        master, moment_one, moment_two, grad_shard, adam_rates, iteration_tally
    )
    new_master = lax.all_gather(new_shard, "zero", axis=0, tiled=True)
    return (tokens_out, grad_tokens, new_master, grad_shard, first_next, second_next)


def solution(mesh):
    return jax.shard_map(
        on_device,
        mesh=mesh,
        in_specs=(
            P("zero", "dp", None),
            P(("dp", "zero"), None, None),
            P(),
            P(),
            P("zero"),
            P("zero"),
            P("zero"),
            P(),
            P(),
        ),
        out_specs=(
            P("zero", "dp", None),
            P("zero", "dp", None),
            P(),
            P("zero"),
            P("zero"),
            P("zero"),
        ),
        check_vma=False,
    )
```

profile of v0, /device:TPU:0, one launch (start us, length us, event | category | flops | bytes accessed | tf_op | source)
XLA Modules:
  0.0 1918.3 jit_solution(2939030028046940159)
XLA Ops:
  18.1 7.3 all-to-all-start
  27.2 68.9 %all-to-all-done = bf16[16,128,768]{2,1,0:T(8,128)(2,1)} async-done(((bf16[16,128,768]{2,1,0:T(8,128)(2,1)}), bf16[16,128,768]{2,1,0:T(8,128)(2,1)}, u32[]{:S(2)}, u32[]{:S(2)}) %all-to-all-start) | async-done | bytes 3145760 | tf_op jit(solution)/shard_map/all_to_all | solution.py:206
  113.8 9.7 reshape.1647
  124.2 11.8 convolution_bitcast_fusion.1
  141.5 9.5 fusion.126
  156.0 8.1 reshape.1649
  178.9 254.5 %while.45 = (s32[]{:T(128)}, f32[1,24,64,128]{3,2,1,0:T(8,128)S(1)}, f32[1]{0:T(128)}, f32[4,1,256,24,64]{2,0,4,3,1:T(4,128)}, f32[4,1,24,64,128]{4,3,2,1,0:T(8,...) while((s32[]{:T(128)}, ...), condition=%wide.region_4.6_spmd.clone, body=%wide.region_1.5_spmd.clone.sunk | while | flops 2526444544 | bytes 20096584 | solution.py:116
  183.2 9.3 fusion.244
  198.4 34.7 %dynamic_update_slice.74 = f32[4,1,256,24,64]{2,0,4,3,1:T(4,128)} dynamic-update-slice(f32[4,1,256,24,64]{2,0,4,3,1:T(4,128)} %get-tuple-element.1165, f32[1,1,256,24,64]{2,0,4,3,1:T(1,128)} %copy.373, s32[]{:T(128)} %get-tuple-element.1162, s32[]{:T(128)} %constant.237.clone.1..sunk, s32[]{:T(128)} %constant.237.clone.1..sunk, s32[]{:T(128)} %constant.237.clone.1..sunk, s32[]{:T(128)} %constant.237.clone.1..sunk) | dynamic-update-slice | bytes 3145732 | tf_op jit(solution)/shard_map/jvp()/while/body/jit(dynamic_update_index_in_dim)/dynamic_update_slice | solution.py:116
  246.7 9.3 fusion.244
  261.9 34.7 %dynamic_update_slice.74 = f32[4,1,256,24,64]{2,0,4,3,1:T(4,128)} dynamic-update-slice(f32[4,1,256,24,64]{2,0,4,3,1:T(4,128)} %get-tuple-element.1165, f32[1,1,256,24,64]{2,0,4,3,1:T(1,128)} %copy.373, s32[]{:T(128)} %get-tuple-element.1162, s32[]{:T(128)} %constant.237.clone.1..sunk, s32[]{:T(128)} %constant.237.clone.1..sunk, s32[]{:T(128)} %constant.237.clone.1..sunk, s32[]{:T(128)} %constant.237.clone.1..sunk) | dynamic-update-slice | bytes 3145732 | tf_op jit(solution)/shard_map/jvp()/while/body/jit(dynamic_update_index_in_dim)/dynamic_update_slice | solution.py:116
  310.4 9.3 fusion.244
  325.6 34.7 %dynamic_update_slice.74 = f32[4,1,256,24,64]{2,0,4,3,1:T(4,128)} dynamic-update-slice(f32[4,1,256,24,64]{2,0,4,3,1:T(4,128)} %get-tuple-element.1165, f32[1,1,256,24,64]{2,0,4,3,1:T(1,128)} %copy.373, s32[]{:T(128)} %get-tuple-element.1162, s32[]{:T(128)} %constant.237.clone.1..sunk, s32[]{:T(128)} %constant.237.clone.1..sunk, s32[]{:T(128)} %constant.237.clone.1..sunk, s32[]{:T(128)} %constant.237.clone.1..sunk) | dynamic-update-slice | bytes 3145732 | tf_op jit(solution)/shard_map/jvp()/while/body/jit(dynamic_update_index_in_dim)/dynamic_update_slice | solution.py:116
  374.0 9.3 fusion.244
  389.1 34.7 %dynamic_update_slice.74 = f32[4,1,256,24,64]{2,0,4,3,1:T(4,128)} dynamic-update-slice(f32[4,1,256,24,64]{2,0,4,3,1:T(4,128)} %get-tuple-element.1165, f32[1,1,256,24,64]{2,0,4,3,1:T(1,128)} %copy.373, s32[]{:T(128)} %get-tuple-element.1162, s32[]{:T(128)} %constant.237.clone.1..sunk, s32[]{:T(128)} %constant.237.clone.1..sunk, s32[]{:T(128)} %constant.237.clone.1..sunk, s32[]{:T(128)} %constant.237.clone.1..sunk) | dynamic-update-slice | bytes 3145732 | tf_op jit(solution)/shard_map/jvp()/while/body/jit(dynamic_update_index_in_dim)/dynamic_update_slice | solution.py:116
  433.4 8.3 transpose.177
  441.9 10.5 multiply_reduce_fusion.8
  458.8 7.9 fusion.131
  466.7 16.1 multiply_reduce_fusion.7
  482.9 8.1 reshape.1657
  497.6 514.2 %while.46 = (s32[]{:T(128)}, f32[24]{0:T(128)}, f32[1,24,64,128]{3,2,1,0:T(8,128)}, f32[4,1,256,24,64]{2,0,4,3,1:T(4,128)}, f32[4,1,256,24]{3,2,1,0:T(8,128)}, /...) while((s32[]{:T(128)}, f32[24]{0:T(128)}, ...), condition=%wide.region_21.24_spmd.clone, body=%wide.region_8.23_spmd.clone.sunk | while | flops 5772160000 | bytes 61074916 | solution.py:116
  533.2 11.8 fusion.264
  587.7 34.7 %dynamic_update_slice.78 = f32[4,1,256,24,64]{2,0,4,3,1:T(4,128)} dynamic-update-slice(f32[4,1,256,24,64]{2,0,4,3,1:T(4,128)} %get-tuple-element.1215, f32[1,1,256,24,64]{2,0,4,3,1:T(1,128)} %copy.392, s32[]{:T(128)S(6)} %sub.331, s32[]{:T(128)} %constant.237.clone.1..sunk.1, s32[]{:T(128)} %constant.237.clone.1..sunk.1, s32[]{:T(128)} %constant.237.clone.1..sunk.1, s32[]{:T(128)} %constant.237.clone.1..sunk.1) | dynamic-update-slice | bytes 3145732 | tf_op jit(solution)/shard_map/transpose(jvp())/while/body/jit(dynamic_update_index_in_dim)/dynamic_update_slice | solution.py:116
  661.8 11.8 fusion.264
  716.4 34.7 %dynamic_update_slice.78 = f32[4,1,256,24,64]{2,0,4,3,1:T(4,128)} dynamic-update-slice(f32[4,1,256,24,64]{2,0,4,3,1:T(4,128)} %get-tuple-element.1215, f32[1,1,256,24,64]{2,0,4,3,1:T(1,128)} %copy.392, s32[]{:T(128)S(6)} %sub.331, s32[]{:T(128)} %constant.237.clone.1..sunk.1, s32[]{:T(128)} %constant.237.clone.1..sunk.1, s32[]{:T(128)} %constant.237.clone.1..sunk.1, s32[]{:T(128)} %constant.237.clone.1..sunk.1) | dynamic-update-slice | bytes 3145732 | tf_op jit(solution)/shard_map/transpose(jvp())/while/body/jit(dynamic_update_index_in_dim)/dynamic_update_slice | solution.py:116
  790.6 11.8 fusion.264
  845.2 34.7 %dynamic_update_slice.78 = f32[4,1,256,24,64]{2,0,4,3,1:T(4,128)} dynamic-update-slice(f32[4,1,256,24,64]{2,0,4,3,1:T(4,128)} %get-tuple-element.1215, f32[1,1,256,24,64]{2,0,4,3,1:T(1,128)} %copy.392, s32[]{:T(128)S(6)} %sub.331, s32[]{:T(128)} %constant.237.clone.1..sunk.1, s32[]{:T(128)} %constant.237.clone.1..sunk.1, s32[]{:T(128)} %constant.237.clone.1..sunk.1, s32[]{:T(128)} %constant.237.clone.1..sunk.1) | dynamic-update-slice | bytes 3145732 | tf_op jit(solution)/shard_map/transpose(jvp())/while/body/jit(dynamic_update_index_in_dim)/dynamic_update_slice | solution.py:116
  919.2 11.8 fusion.264
  973.8 34.7 %dynamic_update_slice.78 = f32[4,1,256,24,64]{2,0,4,3,1:T(4,128)} dynamic-update-slice(f32[4,1,256,24,64]{2,0,4,3,1:T(4,128)} %get-tuple-element.1215, f32[1,1,256,24,64]{2,0,4,3,1:T(1,128)} %copy.392, s32[]{:T(128)S(6)} %sub.331, s32[]{:T(128)} %constant.237.clone.1..sunk.1, s32[]{:T(128)} %constant.237.clone.1..sunk.1, s32[]{:T(128)} %constant.237.clone.1..sunk.1, s32[]{:T(128)} %constant.237.clone.1..sunk.1) | dynamic-update-slice | bytes 3145732 | tf_op jit(solution)/shard_map/transpose(jvp())/while/body/jit(dynamic_update_index_in_dim)/dynamic_update_slice | solution.py:116
  1011.8 8.3 transpose.181
  1020.1 8.0 multiply_add_fusion.1
  1028.7 19.7 %multiply_reduce_fusion.5 = (f32[1792]{0:T(1024)S(1)}, f32[1792]{0:T(1024)S(1)}, f32[1792]{0:T(1024)S(1)}, f32[1792]{0:T(1024)S(1)}, f32[1792]{0:T(1024)S(1)}, /*index=5*/f32[1,1024,1792]{1,2,0:T(8,128)S(1)}) fusion(f32[1,1024,1792]{1,2,0:T(8,128)} %copy-done.6, f32[1024]{0:T(1024)S(1)} %bitcast.707, f32[1024]{0:T(1024)S(1)} %bitcast.701, ...), kind=kLoop, calls=%fused_computation.202 | loop fusion | flops 44031232 | bytes 36752384 | tf_op jit(solution)/shard_map/transpose(jvp())/reduce_sum | solution.py:71
  1048.5 10.5 multiply_multiply_fusion.4
  1060.3 15.0 pad_add_fusion
  1075.3 14.6 fusion.150
  1090.0 12.5 fusion.138
  1102.5 7.6 fusion.145
  1110.2 11.1 reshape.1661
  1128.4 87.9 %dynamic-update-slice.1 = f32[3768320]{0:T(1024)} dynamic-update-slice(f32[3768320]{0:T(1024)} %constant_dynamic-update-slice_fusion.6, f32[2574336]{0:T(1024)} %reshape.1661, s32[]{} %constant.327) | dynamic-update-slice | bytes 20594692
  1224.9 41.0 %dynamic-update-slice.8 = f32[3768320]{0:T(1024)} dynamic-update-slice(f32[3768320]{0:T(1024)} %constant_dynamic-update-slice_fusion, f32[1179648]{0:T(1024)} %reshape.1663, s32[]{} %constant.334) | dynamic-update-slice | bytes 9437188
  1269.1 258.3 %all-reduce.26.cloned.1.call-done = f32[3768320]{0:T(1024)} async-done(((f32[3768320]{0:T(1024)}), f32[3768320]{0:T(1024)}) %all-reduce.26.cloned.1.call-update) | async-done | bytes 15073296
  1533.0 145.1 %all-reduce.24.cloned.1.call-done = f32[942080]{0:T(1024)} async-done(((f32[942080]{0:T(1024)}), f32[942080]{0:T(1024)}) %all-reduce.24.cloned.1.call-update) | async-done | bytes 3768336 | tf_op jit(solution)/shard_map/psum | solution.py:290
  1678.1 11.5 multiply_subtract_fusion
  1695.8 9.4 gather_fusion.3
  1709.0 9.4 gather_fusion.5
  1741.2 66.2 %all-to-all-done.1 = bf16[2,1024,768]{2,0,1:T(2,128)(2,1)} async-done(((bf16[2,1024,768]{2,0,1:T(2,128)(2,1)}), bf16[2,1024,768]{2,0,1:T(2,128)(2,1)}, u32[]{:S(2)}, u32[]{:S(2)}) %all-to-all-start.1) | async-done | bytes 3145760 | tf_op jit(solution)/shard_map/all_to_all | solution.py:268
  1816.1 65.8 %all-to-all-done.2 = bf16[2,1024,768]{2,0,1:T(2,128)(2,1)S(1)} async-done(((bf16[2,1024,768]{2,0,1:T(2,128)(2,1)}), bf16[2,1024,768]{2,0,1:T(2,128)(2,1)S(1)}, u32[]{:S(2)}, u32[]{:S(2)}) %all-to-all-start.2) | async-done | bytes 3145760 | tf_op jit(solution)/shard_map/all_to_all | solution.py:269
  1897.5 11.7 copy.460
  (689 shorter events, 547.8 us)
Async XLA Ops:
  7.2 100.3 %all-gather.3.cloned.1.call-start = ((), (), s32[]{:S(2)}) async-start(), calls=%async_computation.3 | async-start | bytes 9420800 | tf_op jit(solution)/shard_map/all_gather | solution.py:184
  18.1 78.1 %all-to-all-start = ((bf16[16,128,768]{2,1,0:T(8,128)(2,1)}), bf16[16,128,768]{2,1,0:T(8,128)(2,1)}, u32[]{:S(2)}, u32[]{:S(2)}) async-start(bf16[16,128,768]{2,1,0:T(8,128)(2,1)} %broadcast_select_fusion.6), calls=%async_computation | async-start | bytes 6291456 | tf_op jit(solution)/shard_map/all_to_all | solution.py:206
  25.4 1502.0 %all-reduce.26.cloned.1.call-start = ((), (), s32[]{:S(2)}) async-start(), calls=%async_computation.6 | async-start | bytes 30146560
  27.1 97.1 %copy-start.60 = (pred[1024]{0:T(1024)(128)(4,1)}, pred[1024]{0:T(1024)(128)(4,1)S(1)}, u32[]{:S(2)}) copy-start(pred[1024]{0:T(1024)(128)(4,1)S(1)} %get-tuple-element.907) | copy-start | bytes 3076
  27.1 114.4 %copy-start.33 = (f32[1024]{0:T(1024)}, f32[1024]{0:T(1024)S(1)}, u32[]{:S(2)}) copy-start(f32[1024]{0:T(1024)S(1)} %get-tuple-element.908) | copy-start | bytes 12292
  27.2 114.3 %copy-start.35 = (f32[1,1024]{1,0:T(1,128)}, f32[1,1024]{1,0:T(1,128)S(1)}, u32[]{:S(2)}) copy-start(f32[1,1024]{1,0:T(1,128)S(1)} %get-tuple-element.896) | copy-start | bytes 12292
  27.2 114.3 %copy-start.37 = (f32[1,1024]{1,0:T(1,128)}, f32[1,1024]{1,0:T(1,128)S(1)}, u32[]{:S(2)}) copy-start(f32[1,1024]{1,0:T(1,128)S(1)} %get-tuple-element.897) | copy-start | bytes 12292
  27.2 114.3 %copy-start.39 = (f32[1,1024]{1,0:T(1,128)}, f32[1,1024]{1,0:T(1,128)S(1)}, u32[]{:S(2)}) copy-start(f32[1,1024]{1,0:T(1,128)S(1)} %get-tuple-element.898) | copy-start | bytes 12292
  106.8 17.4 copy-start.9
  107.5 16.0 copy-start.43
  107.5 16.7 copy-start.50
  441.9 24.8 %copy-start.23 = (f32[1536]{0:T(1024)}, f32[1536]{0:T(1024)S(1)}, u32[]{:S(2)}) copy-start(f32[1536]{0:T(1024)S(1)} %mul.958) | copy-start | bytes 18436
  497.7 14.7 copy-start.41
  577.7 44.8 %copy-start.18 = (f32[256,24]{0,1:T(8,128)S(1)}, f32[256,24]{0,1:T(8,128)}, u32[]{:S(2)}) copy-start(f32[256,24]{0,1:T(8,128)} %copy.390) | copy-start | bytes 73732 | tf_op jit(solution)/shard_map/transpose(jvp())/while
  584.8 39.9 %copy-start.57 = (f32[24]{0:T(128)S(1)}, f32[24]{0:T(128)}, u32[]{:S(2)}) copy-start(f32[24]{0:T(128)} %get-tuple-element.1213) | copy-start | bytes 292 | tf_op jit(solution)/shard_map/transpose(jvp())/while
  584.8 40.4 %copy-start.16 = (f32[4,1,256,128]{3,2,1,0:T(8,128)S(1)}, f32[4,1,256,128]{3,2,1,0:T(8,128)}, u32[]{:S(2)}) copy-start(f32[4,1,256,128]{3,2,1,0:T(8,128)} %copy-done.15) | copy-start | bytes 1572868 | tf_op jit(solution)/shard_map/transpose(jvp())/while
  584.9 40.4 %copy-start.42 = (f32[24]{0:T(128)S(1)}, f32[24]{0:T(128)}, u32[]{:S(2)}) copy-start(f32[24]{0:T(128)} %copy-done.41) | copy-start | bytes 292 | tf_op jit(solution)/shard_map/transpose(jvp())/while
  625.3 15.9 copy-start.41
  706.3 44.8 %copy-start.18 = (f32[256,24]{0,1:T(8,128)S(1)}, f32[256,24]{0,1:T(8,128)}, u32[]{:S(2)}) copy-start(f32[256,24]{0,1:T(8,128)} %copy.390) | copy-start | bytes 73732 | tf_op jit(solution)/shard_map/transpose(jvp())/while
  713.5 39.9 %copy-start.57 = (f32[24]{0:T(128)S(1)}, f32[24]{0:T(128)}, u32[]{:S(2)}) copy-start(f32[24]{0:T(128)} %get-tuple-element.1213) | copy-start | bytes 292 | tf_op jit(solution)/shard_map/transpose(jvp())/while
  713.5 40.4 %copy-start.16 = (f32[4,1,256,128]{3,2,1,0:T(8,128)S(1)}, f32[4,1,256,128]{3,2,1,0:T(8,128)}, u32[]{:S(2)}) copy-start(f32[4,1,256,128]{3,2,1,0:T(8,128)} %copy-done.15) | copy-start | bytes 1572868 | tf_op jit(solution)/shard_map/transpose(jvp())/while
  713.6 40.4 %copy-start.42 = (f32[24]{0:T(128)S(1)}, f32[24]{0:T(128)}, u32[]{:S(2)}) copy-start(f32[24]{0:T(128)} %copy-done.41) | copy-start | bytes 292 | tf_op jit(solution)/shard_map/transpose(jvp())/while
  754.0 15.9 copy-start.41
  835.1 44.8 %copy-start.18 = (f32[256,24]{0,1:T(8,128)S(1)}, f32[256,24]{0,1:T(8,128)}, u32[]{:S(2)}) copy-start(f32[256,24]{0,1:T(8,128)} %copy.390) | copy-start | bytes 73732 | tf_op jit(solution)/shard_map/transpose(jvp())/while
  842.3 39.9 %copy-start.57 = (f32[24]{0:T(128)S(1)}, f32[24]{0:T(128)}, u32[]{:S(2)}) copy-start(f32[24]{0:T(128)} %get-tuple-element.1213) | copy-start | bytes 292 | tf_op jit(solution)/shard_map/transpose(jvp())/while
  842.3 40.4 %copy-start.16 = (f32[4,1,256,128]{3,2,1,0:T(8,128)S(1)}, f32[4,1,256,128]{3,2,1,0:T(8,128)}, u32[]{:S(2)}) copy-start(f32[4,1,256,128]{3,2,1,0:T(8,128)} %copy-done.15) | copy-start | bytes 1572868 | tf_op jit(solution)/shard_map/transpose(jvp())/while
  842.3 40.4 %copy-start.42 = (f32[24]{0:T(128)S(1)}, f32[24]{0:T(128)}, u32[]{:S(2)}) copy-start(f32[24]{0:T(128)} %copy-done.41) | copy-start | bytes 292 | tf_op jit(solution)/shard_map/transpose(jvp())/while
  882.7 15.8 copy-start.41
  963.8 44.8 %copy-start.18 = (f32[256,24]{0,1:T(8,128)S(1)}, f32[256,24]{0,1:T(8,128)}, u32[]{:S(2)}) copy-start(f32[256,24]{0,1:T(8,128)} %copy.390) | copy-start | bytes 73732 | tf_op jit(solution)/shard_map/transpose(jvp())/while
  970.9 39.9 %copy-start.57 = (f32[24]{0:T(128)S(1)}, f32[24]{0:T(128)}, u32[]{:S(2)}) copy-start(f32[24]{0:T(128)} %get-tuple-element.1213) | copy-start | bytes 292 | tf_op jit(solution)/shard_map/transpose(jvp())/while
  971.0 40.4 %copy-start.16 = (f32[4,1,256,128]{3,2,1,0:T(8,128)S(1)}, f32[4,1,256,128]{3,2,1,0:T(8,128)}, u32[]{:S(2)}) copy-start(f32[4,1,256,128]{3,2,1,0:T(8,128)} %copy-done.15) | copy-start | bytes 1572868 | tf_op jit(solution)/shard_map/transpose(jvp())/while
  971.0 40.4 %copy-start.42 = (f32[24]{0:T(128)S(1)}, f32[24]{0:T(128)}, u32[]{:S(2)}) copy-start(f32[24]{0:T(128)} %copy-done.41) | copy-start | bytes 292 | tf_op jit(solution)/shard_map/transpose(jvp())/while
  1028.7 19.7 %copy-start.26 = (f32[1792]{0:T(1024)S(1)}, f32[1792]{0:T(1024)}, u32[]{:S(2)}) copy-start(f32[1792]{0:T(1024)} %copy-done.25) | copy-start | bytes 21508
  1028.7 19.7 %copy-start.28 = (f32[1792]{0:T(1024)S(1)}, f32[1792]{0:T(1024)}, u32[]{:S(2)}) copy-start(f32[1792]{0:T(1024)} %copy-done.27) | copy-start | bytes 21508
  1028.7 19.7 %copy-start.30 = (f32[1792]{0:T(1024)S(1)}, f32[1792]{0:T(1024)}, u32[]{:S(2)}) copy-start(f32[1792]{0:T(1024)} %copy-done.29) | copy-start | bytes 21508
  1028.7 19.7 %copy-start.32 = (f32[1792]{0:T(1024)S(1)}, f32[1792]{0:T(1024)}, u32[]{:S(2)}) copy-start(f32[1792]{0:T(1024)} %copy-done.31) | copy-start | bytes 21508
  1060.3 15.0 copy-start.10
  1060.3 15.0 copy-start.51
  1060.3 15.0 copy-start.53
  1060.3 15.0 copy-start.61
  1128.4 91.9 %copy-start.59 = (f32[24]{0:T(128)S(1)}, f32[24]{0:T(128)}, u32[]{:S(2)}) copy-start(f32[24]{0:T(128)} %get-tuple-element.474) | copy-start | bytes 292
  1128.4 95.2 %copy-start.62 = (f32[1536]{0:T(1024)S(1)}, f32[1536]{0:T(1024)}, u32[]{:S(2)}) copy-start(f32[1536]{0:T(1024)} %get-tuple-element.783) | copy-start | bytes 18436
  1267.2 265.1 %copy-start.65 = (f32[2]{0:T(128)S(1)}, f32[2]{0:T(128)}, u32[]{:S(2)}) copy-start(f32[2]{0:T(128)} %param.24) | copy-start | bytes 28
  1267.3 410.9 %all-reduce.24.cloned.1.call-start = ((), (), s32[]{:S(2)}) async-start(), calls=%async_computation.4 | async-start | bytes 7536640 | tf_op jit(solution)/shard_map/psum | solution.py:290
  1531.6 365.9 %all-gather.5.cloned.1.call-start = ((), (), s32[]{:S(2)}) async-start(), calls=%async_computation.5 | async-start | bytes 18841600 | tf_op jit(solution)/shard_map/all_gather | solution.py:294
  1731.6 75.9 %all-to-all-start.1 = ((bf16[2,1024,768]{2,0,1:T(2,128)(2,1)}), bf16[2,1024,768]{2,0,1:T(2,128)(2,1)}, u32[]{:S(2)}, u32[]{:S(2)}) async-start(bf16[2,1024,768]{2,0,1:T(2,128)(2,1)} %copy.241), calls=%async_computation.1 | async-start | bytes 6291456 | tf_op jit(solution)/shard_map/all_to_all | solution.py:268
  1736.3 74.8 %copy-start.56 = (s32[8,2]{1,0:T(8,128)S(1)}, s32[8,2]{1,0:T(8,128)}, u32[]{:S(2)}) copy-start(s32[8,2]{1,0:T(8,128)} %get-tuple-element.789) | copy-start | bytes 196
  1807.4 74.5 %all-to-all-start.2 = ((bf16[2,1024,768]{2,0,1:T(2,128)(2,1)}), bf16[2,1024,768]{2,0,1:T(2,128)(2,1)S(1)}, u32[]{:S(2)}, u32[]{:S(2)}) async-start(bf16[2,1024,768]{2,0,1:T(2,128)(2,1)} %copy.255), calls=%async_computation.2 | async-start | bytes 6291456 | tf_op jit(solution)/shard_map/all_to_all | solution.py:269
  (60 other events, 475.6 us)
Sparse Core Ops, SparseCore 0:
  11.0 56.1 all-gather.2
  1267.4 259.9 all-reduce.25
  1532.1 145.9 all-reduce.23
  1689.8 95.2 all-gather.4
where the time goes:
time: 1950 us; the launch traced here: 1920 us
  local copies, waits for them, and re-layouts  772 us (40%)
  waiting for transfers between devices  604 us (31%)
  matrix products  276 us (14%)
  other arithmetic  221 us (11%)
    dynamic_update_slice x28, local copies, waits for them, and re-layouts, span_scan(): lax.scan(jax.checkpoint(advance), initial, (split_blocks(x_heads), split_...  324 us
    unnamed x5, waiting for transfers between devices  258 us
    unnamed x130, local copies, waits for them, and re-layouts  167 us
    psum x1, waiting for transfers between devices, on_device(): grad_shard = lax.psum(grad_shard, 'dp')  145 us
    dot_general x12, matrix products, advance(): jnp.einsum('shtr,srhp->sthp', mixing, x_blk, precision=EXACT_MATMUL)  113 us
    all_to_all x1, waiting for transfers between devices, on_device(): lax.all_to_all(dealt_rows, 'dp', split_axis=0, concat_axis=1, tiled=True)  68.9 us
    all_to_all x1, waiting for transfers between devices, on_device(): lax.all_to_all(result, 'dp', split_axis=1, concat_axis=0, tiled=True)  66.2 us
    all_to_all x1, waiting for transfers between devices, on_device(): lax.all_to_all(grad_input, 'dp', split_axis=1, concat_axis=0, tiled=True)  65.8 us
  transfers between devices with their start and end apart: 7, of which 5 were waited for; matrix products, arithmetic and copies ran while one was open for 5% of the time, Pallas kernels for 0%

commit v1 on v0

--- a/solution.py
+++ b/solution.py
@@ -1,3 +1,4 @@
+import functools
 from functools import partial
 import jax
 import jax.numpy as jnp
@@ -18,6 +19,13 @@
 BETA_ONE = 0.9
 BETA_TWO = 0.95
 EPS_ADAM = 1e-08
+
+
+def plan_view(local_x, net_axis):
+    return jnp.sum(lax.all_gather(local_x, net_axis), axis=0)
+
+
+_hold_sides = functools.partial(plan_view, net_axis="dp")
 
 
 def padded_slot(amount):
@@ -287,7 +295,7 @@
     used_len = sum((piece.shape[0] for piece in laid))
     flat_grad = jnp.concatenate(laid + [jnp.zeros((vector_len - used_len,), jnp.float32)])
     grad_shard = lax.psum_scatter(flat_grad, "zero", scatter_dimension=0, tiled=True)
-    grad_shard = lax.psum(grad_shard, "dp")
+    grad_shard = _hold_sides(grad_shard)
     new_shard, first_next, second_next = adam_update(
         master, moment_one, moment_two, grad_shard, adam_rates, iteration_tally
     )

time: 1950 us -> 2450 us (1.26)
  waiting for transfers between devices: 604 us -> 1030 us
  other arithmetic: 221 us -> 264 us
    all_gather x0 -> x1, waiting for transfers between devices: none -> 573 us  [plan_view(): return jnp.sum(lax.all_gather(local_x, net_axis), axis=0)]
    psum x1 -> x0, waiting for transfers between devices: 145 us -> none  [on_device(): grad_shard = lax.psum(grad_shard, 'dp')]
    reduce_sum x0 -> x1, other arithmetic: none -> 42.8 us  [plan_view(): return jnp.sum(lax.all_gather(local_x, net_axis), axis=0)]
    all_gather x0 -> x1, local copies, waits for them, and re-layouts: none -> 26.6 us  [plan_view(): return jnp.sum(lax.all_gather(local_x, net_axis), axis=0)]
    unnamed x130 -> x127, local copies, waits for them, and re-layouts: 167 us -> 164 us
  transfers between devices with their start and end apart: 7 -> 7, of which waited for: 5 -> 5; matrix products, arithmetic and copies ran while one was open for 5% -> 4% of each run, Pallas kernels for 0% -> 0%
where the time goes in v1:
time: 2450 us; the launch traced here: 2410 us
  waiting for transfers between devices  1030 us (42%)
  local copies, waits for them, and re-layouts  795 us (32%)
  matrix products  276 us (11%)
  other arithmetic  264 us (11%)
    all_gather x1, waiting for transfers between devices, plan_view(): return jnp.sum(lax.all_gather(local_x, net_axis), axis=0)  573 us
    dynamic_update_slice x28, local copies, waits for them, and re-layouts, span_scan(): lax.scan(jax.checkpoint(advance), initial, (split_blocks(x_heads), split_...  324 us
    unnamed x5, waiting for transfers between devices  258 us
    unnamed x127, local copies, waits for them, and re-layouts  164 us
    dot_general x12, matrix products, advance(): jnp.einsum('shtr,srhp->sthp', mixing, x_blk, precision=EXACT_MATMUL)  113 us
    all_to_all x1, waiting for transfers between devices, on_device(): lax.all_to_all(dealt_rows, 'dp', split_axis=0, concat_axis=1, tiled=True)  68.9 us
    all_to_all x1, waiting for transfers between devices, on_device(): lax.all_to_all(result, 'dp', split_axis=1, concat_axis=0, tiled=True)  66.2 us
    all_to_all x1, waiting for transfers between devices, on_device(): lax.all_to_all(grad_input, 'dp', split_axis=1, concat_axis=0, tiled=True)  65.9 us
  transfers between devices with their start and end apart: 7, of which 5 were waited for; matrix products, arithmetic and copies ran while one was open for 4% of the time, Pallas kernels for 0%

profile of v1, /device:TPU:0, one launch (start us, length us, event | category | flops | bytes accessed | tf_op | source)
XLA Modules:
  0.0 2412.4 jit_solution(2115502807775639696)
XLA Ops:
  27.3 68.9 %all-to-all-done = bf16[16,128,768]{2,1,0:T(8,128)(2,1)} async-done(((bf16[16,128,768]{2,1,0:T(8,128)(2,1)}), bf16[16,128,768]{2,1,0:T(8,128)(2,1)}, u32[]{:S(2)}, u32[]{:S(2)}) %all-to-all-start) | async-done | bytes 3145760 | tf_op jit(solution)/shard_map/all_to_all | solution.py:214
  113.7 9.7 reshape.1647
  124.2 11.7 convolution_bitcast_fusion.1
  141.4 9.6 fusion.126
  156.0 8.1 reshape.1649
  179.0 255.2 %while.45 = (s32[]{:T(128)}, f32[1,24,64,128]{3,2,1,0:T(8,128)S(1)}, f32[1]{0:T(128)}, f32[4,1,256,24,64]{2,0,4,3,1:T(4,128)}, f32[4,1,24,64,128]{4,3,2,1,0:T(8,...) while((s32[]{:T(128)}, ...), condition=%wide.region_4.6_spmd.clone, body=%wide.region_1.5_spmd.clone.sunk | while | flops 2526444544 | bytes 20096584 | solution.py:124
  183.6 9.3 fusion.244
  198.8 34.7 %dynamic_update_slice.74 = f32[4,1,256,24,64]{2,0,4,3,1:T(4,128)} dynamic-update-slice(f32[4,1,256,24,64]{2,0,4,3,1:T(4,128)} %get-tuple-element.1165, f32[1,1,256,24,64]{2,0,4,3,1:T(1,128)} %copy.374, s32[]{:T(128)} %get-tuple-element.1162, s32[]{:T(128)} %constant.237.clone.1..sunk, s32[]{:T(128)} %constant.237.clone.1..sunk, s32[]{:T(128)} %constant.237.clone.1..sunk, s32[]{:T(128)} %constant.237.clone.1..sunk) | dynamic-update-slice | bytes 3145732 | tf_op jit(solution)/shard_map/jvp()/while/body/jit(dynamic_update_index_in_dim)/dynamic_update_slice | solution.py:124
  247.3 9.3 fusion.244
  262.5 34.7 %dynamic_update_slice.74 = f32[4,1,256,24,64]{2,0,4,3,1:T(4,128)} dynamic-update-slice(f32[4,1,256,24,64]{2,0,4,3,1:T(4,128)} %get-tuple-element.1165, f32[1,1,256,24,64]{2,0,4,3,1:T(1,128)} %copy.374, s32[]{:T(128)} %get-tuple-element.1162, s32[]{:T(128)} %constant.237.clone.1..sunk, s32[]{:T(128)} %constant.237.clone.1..sunk, s32[]{:T(128)} %constant.237.clone.1..sunk, s32[]{:T(128)} %constant.237.clone.1..sunk) | dynamic-update-slice | bytes 3145732 | tf_op jit(solution)/shard_map/jvp()/while/body/jit(dynamic_update_index_in_dim)/dynamic_update_slice | solution.py:124
  311.1 9.3 fusion.244
  326.3 34.7 %dynamic_update_slice.74 = f32[4,1,256,24,64]{2,0,4,3,1:T(4,128)} dynamic-update-slice(f32[4,1,256,24,64]{2,0,4,3,1:T(4,128)} %get-tuple-element.1165, f32[1,1,256,24,64]{2,0,4,3,1:T(1,128)} %copy.374, s32[]{:T(128)} %get-tuple-element.1162, s32[]{:T(128)} %constant.237.clone.1..sunk, s32[]{:T(128)} %constant.237.clone.1..sunk, s32[]{:T(128)} %constant.237.clone.1..sunk, s32[]{:T(128)} %constant.237.clone.1..sunk) | dynamic-update-slice | bytes 3145732 | tf_op jit(solution)/shard_map/jvp()/while/body/jit(dynamic_update_index_in_dim)/dynamic_update_slice | solution.py:124
  374.7 9.3 fusion.244
  389.9 34.7 %dynamic_update_slice.74 = f32[4,1,256,24,64]{2,0,4,3,1:T(4,128)} dynamic-update-slice(f32[4,1,256,24,64]{2,0,4,3,1:T(4,128)} %get-tuple-element.1165, f32[1,1,256,24,64]{2,0,4,3,1:T(1,128)} %copy.374, s32[]{:T(128)} %get-tuple-element.1162, s32[]{:T(128)} %constant.237.clone.1..sunk, s32[]{:T(128)} %constant.237.clone.1..sunk, s32[]{:T(128)} %constant.237.clone.1..sunk, s32[]{:T(128)} %constant.237.clone.1..sunk) | dynamic-update-slice | bytes 3145732 | tf_op jit(solution)/shard_map/jvp()/while/body/jit(dynamic_update_index_in_dim)/dynamic_update_slice | solution.py:124
  434.3 8.3 transpose.177
  442.7 10.4 multiply_reduce_fusion.8
  459.2 7.9 fusion.131
  467.2 16.1 multiply_reduce_fusion.7
  483.2 8.1 reshape.1657
  497.9 513.7 %while.46 = (s32[]{:T(128)}, f32[24]{0:T(128)}, f32[1,24,64,128]{3,2,1,0:T(8,128)}, f32[4,1,256,24,64]{2,0,4,3,1:T(4,128)}, f32[4,1,256,24]{3,2,1,0:T(8,128)}, /...) while((s32[]{:T(128)}, f32[24]{0:T(128)}, ...), condition=%wide.region_21.24_spmd.clone, body=%wide.region_8.23_spmd.clone.sunk | while | flops 5772160000 | bytes 61074916 | solution.py:124
  533.5 11.8 fusion.264
  588.1 34.7 %dynamic_update_slice.78 = f32[4,1,256,24,64]{2,0,4,3,1:T(4,128)} dynamic-update-slice(f32[4,1,256,24,64]{2,0,4,3,1:T(4,128)} %get-tuple-element.1215, f32[1,1,256,24,64]{2,0,4,3,1:T(1,128)} %copy.393, s32[]{:T(128)S(6)} %sub.331, s32[]{:T(128)} %constant.237.clone.1..sunk.1, s32[]{:T(128)} %constant.237.clone.1..sunk.1, s32[]{:T(128)} %constant.237.clone.1..sunk.1, s32[]{:T(128)} %constant.237.clone.1..sunk.1) | dynamic-update-slice | bytes 3145732 | tf_op jit(solution)/shard_map/transpose(jvp())/while/body/jit(dynamic_update_index_in_dim)/dynamic_update_slice | solution.py:124
  662.1 11.8 fusion.264
  716.6 34.7 %dynamic_update_slice.78 = f32[4,1,256,24,64]{2,0,4,3,1:T(4,128)} dynamic-update-slice(f32[4,1,256,24,64]{2,0,4,3,1:T(4,128)} %get-tuple-element.1215, f32[1,1,256,24,64]{2,0,4,3,1:T(1,128)} %copy.393, s32[]{:T(128)S(6)} %sub.331, s32[]{:T(128)} %constant.237.clone.1..sunk.1, s32[]{:T(128)} %constant.237.clone.1..sunk.1, s32[]{:T(128)} %constant.237.clone.1..sunk.1, s32[]{:T(128)} %constant.237.clone.1..sunk.1) | dynamic-update-slice | bytes 3145732 | tf_op jit(solution)/shard_map/transpose(jvp())/while/body/jit(dynamic_update_index_in_dim)/dynamic_update_slice | solution.py:124
  790.7 11.8 fusion.264
  845.2 34.7 %dynamic_update_slice.78 = f32[4,1,256,24,64]{2,0,4,3,1:T(4,128)} dynamic-update-slice(f32[4,1,256,24,64]{2,0,4,3,1:T(4,128)} %get-tuple-element.1215, f32[1,1,256,24,64]{2,0,4,3,1:T(1,128)} %copy.393, s32[]{:T(128)S(6)} %sub.331, s32[]{:T(128)} %constant.237.clone.1..sunk.1, s32[]{:T(128)} %constant.237.clone.1..sunk.1, s32[]{:T(128)} %constant.237.clone.1..sunk.1, s32[]{:T(128)} %constant.237.clone.1..sunk.1) | dynamic-update-slice | bytes 3145732 | tf_op jit(solution)/shard_map/transpose(jvp())/while/body/jit(dynamic_update_index_in_dim)/dynamic_update_slice | solution.py:124
  919.3 11.8 fusion.264
  973.8 34.7 %dynamic_update_slice.78 = f32[4,1,256,24,64]{2,0,4,3,1:T(4,128)} dynamic-update-slice(f32[4,1,256,24,64]{2,0,4,3,1:T(4,128)} %get-tuple-element.1215, f32[1,1,256,24,64]{2,0,4,3,1:T(1,128)} %copy.393, s32[]{:T(128)S(6)} %sub.331, s32[]{:T(128)} %constant.237.clone.1..sunk.1, s32[]{:T(128)} %constant.237.clone.1..sunk.1, s32[]{:T(128)} %constant.237.clone.1..sunk.1, s32[]{:T(128)} %constant.237.clone.1..sunk.1) | dynamic-update-slice | bytes 3145732 | tf_op jit(solution)/shard_map/transpose(jvp())/while/body/jit(dynamic_update_index_in_dim)/dynamic_update_slice | solution.py:124
  1011.6 8.3 transpose.181
  1019.9 7.9 multiply_add_fusion.1
  1028.4 19.6 multiply_reduce_fusion.5
  1048.1 10.5 multiply_multiply_fusion.4
  1060.0 15.0 pad_add_fusion
  1075.1 14.5 fusion.150
  1089.6 12.5 fusion.138
  1110.0 11.1 reshape.1661
  1128.2 87.9 %dynamic-update-slice.1 = f32[3768320]{0:T(1024)} dynamic-update-slice(f32[3768320]{0:T(1024)} %constant_dynamic-update-slice_fusion.6, f32[2574336]{0:T(1024)} %reshape.1661, s32[]{} %constant.327) | dynamic-update-slice | bytes 20594692
  1224.8 41.0 %dynamic-update-slice.8 = f32[3768320]{0:T(1024)} dynamic-update-slice(f32[3768320]{0:T(1024)} %constant_dynamic-update-slice_fusion, f32[1179648]{0:T(1024)} %reshape.1663, s32[]{} %constant.334) | dynamic-update-slice | bytes 9437188
  1268.9 258.3 %all-reduce.23.cloned.1.call-done = f32[3768320]{0:T(1024)} async-done(((f32[3768320]{0:T(1024)}), f32[3768320]{0:T(1024)}) %all-reduce.23.cloned.1.call-update) | async-done | bytes 15073296
  1532.8 572.8 %all-gather.9.cloned.1.call-done = f32[7536640]{0:T(1024)} async-done(((f32[942080]{0:T(1024)}), f32[7536640]{0:T(1024)}) %all-gather.9.cloned.1.call-update) | async-done | bytes 30146576 | tf_op jit(solution)/shard_map/all_gather | solution.py:25
  2105.7 26.6 %reshape.1737 = f32[8,942080]{1,0:T(8,128)} reshape(f32[7536640]{0:T(1024)} %all-gather.9.cloned.1.call-done) | data formatting | bytes 60293120 | tf_op jit(solution)/shard_map/all_gather | solution.py:25
  2132.2 42.8 %reduce_sum.247 = f32[942080]{0:T(1024)} reduce(f32[8,942080]{1,0:T(8,128)} %reshape.1737, f32[]{:T(128)} %constant.241.clone.1), dimensions={0}, to_apply=%region_34.37 | reduce | flops 6594560 | bytes 33914884 | tf_op jit(solution)/shard_map/reduce_sum | solution.py:25
  2175.0 11.6 multiply_subtract_fusion
  2192.8 9.5 gather_fusion.3
  2206.3 9.4 gather_fusion.5
  2238.7 66.2 %all-to-all-done.1 = bf16[2,1024,768]{2,0,1:T(2,128)(2,1)} async-done(((bf16[2,1024,768]{2,0,1:T(2,128)(2,1)}), bf16[2,1024,768]{2,0,1:T(2,128)(2,1)}, u32[]{:S(2)}, u32[]{:S(2)}) %all-to-all-start.1) | async-done | bytes 3145760 | tf_op jit(solution)/shard_map/all_to_all | solution.py:276
  2313.5 65.9 %all-to-all-done.2 = bf16[2,1024,768]{2,0,1:T(2,128)(2,1)S(1)} async-done(((bf16[2,1024,768]{2,0,1:T(2,128)(2,1)}), bf16[2,1024,768]{2,0,1:T(2,128)(2,1)S(1)}, u32[]{:S(2)}, u32[]{:S(2)}) %all-to-all-start.2) | async-done | bytes 3145760 | tf_op jit(solution)/shard_map/all_to_all | solution.py:277
  2394.9 10.8 copy.461
  (688 shorter events, 561.1 us)
Async XLA Ops:
  7.2 100.3 %all-gather.5.cloned.1.call-start = ((), (), s32[]{:S(2)}) async-start(), calls=%async_computation.3 | async-start | bytes 9420800 | tf_op jit(solution)/shard_map/all_gather | solution.py:192
  18.1 78.1 %all-to-all-start = ((bf16[16,128,768]{2,1,0:T(8,128)(2,1)}), bf16[16,128,768]{2,1,0:T(8,128)(2,1)}, u32[]{:S(2)}, u32[]{:S(2)}) async-start(bf16[16,128,768]{2,1,0:T(8,128)(2,1)} %broadcast_select_fusion.6), calls=%async_computation | async-start | bytes 6291456 | tf_op jit(solution)/shard_map/all_to_all | solution.py:214
  25.4 1501.8 %all-reduce.23.cloned.1.call-start = ((), (), s32[]{:S(2)}) async-start(), calls=%async_computation.6 | async-start | bytes 30146560
  27.1 97.1 %copy-start.59 = (pred[1024]{0:T(1024)(128)(4,1)}, pred[1024]{0:T(1024)(128)(4,1)S(1)}, u32[]{:S(2)}) copy-start(pred[1024]{0:T(1024)(128)(4,1)S(1)} %get-tuple-element.907) | copy-start | bytes 3076
  27.1 114.3 %copy-start.32 = (f32[1024]{0:T(1024)}, f32[1024]{0:T(1024)S(1)}, u32[]{:S(2)}) copy-start(f32[1024]{0:T(1024)S(1)} %get-tuple-element.908) | copy-start | bytes 12292
  27.2 114.2 %copy-start.34 = (f32[1,1024]{1,0:T(1,128)}, f32[1,1024]{1,0:T(1,128)S(1)}, u32[]{:S(2)}) copy-start(f32[1,1024]{1,0:T(1,128)S(1)} %get-tuple-element.896) | copy-start | bytes 12292
  27.2 114.2 %copy-start.36 = (f32[1,1024]{1,0:T(1,128)}, f32[1,1024]{1,0:T(1,128)S(1)}, u32[]{:S(2)}) copy-start(f32[1,1024]{1,0:T(1,128)S(1)} %get-tuple-element.897) | copy-start | bytes 12292
  27.2 114.2 %copy-start.38 = (f32[1,1024]{1,0:T(1,128)}, f32[1,1024]{1,0:T(1,128)S(1)}, u32[]{:S(2)}) copy-start(f32[1,1024]{1,0:T(1,128)S(1)} %get-tuple-element.898) | copy-start | bytes 12292
  106.8 17.3 copy-start.8
  107.5 16.0 copy-start.42
  107.5 16.6 copy-start.49
  442.7 24.5 %copy-start.22 = (f32[1536]{0:T(1024)}, f32[1536]{0:T(1024)S(1)}, u32[]{:S(2)}) copy-start(f32[1536]{0:T(1024)S(1)} %mul.958) | copy-start | bytes 18436
  498.3 14.7 copy-start.40
  578.0 44.8 %copy-start.17 = (f32[256,24]{0,1:T(8,128)S(1)}, f32[256,24]{0,1:T(8,128)}, u32[]{:S(2)}) copy-start(f32[256,24]{0,1:T(8,128)} %copy.391) | copy-start | bytes 73732 | tf_op jit(solution)/shard_map/transpose(jvp())/while
  585.2 39.9 %copy-start.56 = (f32[24]{0:T(128)S(1)}, f32[24]{0:T(128)}, u32[]{:S(2)}) copy-start(f32[24]{0:T(128)} %get-tuple-element.1213) | copy-start | bytes 292 | tf_op jit(solution)/shard_map/transpose(jvp())/while
  585.2 40.5 %copy-start.15 = (f32[4,1,256,128]{3,2,1,0:T(8,128)S(1)}, f32[4,1,256,128]{3,2,1,0:T(8,128)}, u32[]{:S(2)}) copy-start(f32[4,1,256,128]{3,2,1,0:T(8,128)} %copy-done.14) | copy-start | bytes 1572868 | tf_op jit(solution)/shard_map/transpose(jvp())/while
  585.2 40.5 %copy-start.41 = (f32[24]{0:T(128)S(1)}, f32[24]{0:T(128)}, u32[]{:S(2)}) copy-start(f32[24]{0:T(128)} %copy-done.40) | copy-start | bytes 292 | tf_op jit(solution)/shard_map/transpose(jvp())/while
  625.7 15.8 copy-start.40
  706.5 44.8 %copy-start.17 = (f32[256,24]{0,1:T(8,128)S(1)}, f32[256,24]{0,1:T(8,128)}, u32[]{:S(2)}) copy-start(f32[256,24]{0,1:T(8,128)} %copy.391) | copy-start | bytes 73732 | tf_op jit(solution)/shard_map/transpose(jvp())/while
  713.7 39.9 %copy-start.56 = (f32[24]{0:T(128)S(1)}, f32[24]{0:T(128)}, u32[]{:S(2)}) copy-start(f32[24]{0:T(128)} %get-tuple-element.1213) | copy-start | bytes 292 | tf_op jit(solution)/shard_map/transpose(jvp())/while
  713.7 40.5 %copy-start.15 = (f32[4,1,256,128]{3,2,1,0:T(8,128)S(1)}, f32[4,1,256,128]{3,2,1,0:T(8,128)}, u32[]{:S(2)}) copy-start(f32[4,1,256,128]{3,2,1,0:T(8,128)} %copy-done.14) | copy-start | bytes 1572868 | tf_op jit(solution)/shard_map/transpose(jvp())/while
  713.7 40.5 %copy-start.41 = (f32[24]{0:T(128)S(1)}, f32[24]{0:T(128)}, u32[]{:S(2)}) copy-start(f32[24]{0:T(128)} %copy-done.40) | copy-start | bytes 292 | tf_op jit(solution)/shard_map/transpose(jvp())/while
  754.2 15.9 copy-start.40
  835.1 44.8 %copy-start.17 = (f32[256,24]{0,1:T(8,128)S(1)}, f32[256,24]{0,1:T(8,128)}, u32[]{:S(2)}) copy-start(f32[256,24]{0,1:T(8,128)} %copy.391) | copy-start | bytes 73732 | tf_op jit(solution)/shard_map/transpose(jvp())/while
  842.3 39.9 %copy-start.56 = (f32[24]{0:T(128)S(1)}, f32[24]{0:T(128)}, u32[]{:S(2)}) copy-start(f32[24]{0:T(128)} %get-tuple-element.1213) | copy-start | bytes 292 | tf_op jit(solution)/shard_map/transpose(jvp())/while
  842.3 40.5 %copy-start.15 = (f32[4,1,256,128]{3,2,1,0:T(8,128)S(1)}, f32[4,1,256,128]{3,2,1,0:T(8,128)}, u32[]{:S(2)}) copy-start(f32[4,1,256,128]{3,2,1,0:T(8,128)} %copy-done.14) | copy-start | bytes 1572868 | tf_op jit(solution)/shard_map/transpose(jvp())/while
  842.3 40.5 %copy-start.41 = (f32[24]{0:T(128)S(1)}, f32[24]{0:T(128)}, u32[]{:S(2)}) copy-start(f32[24]{0:T(128)} %copy-done.40) | copy-start | bytes 292 | tf_op jit(solution)/shard_map/transpose(jvp())/while
  882.8 15.9 copy-start.40
  963.8 44.8 %copy-start.17 = (f32[256,24]{0,1:T(8,128)S(1)}, f32[256,24]{0,1:T(8,128)}, u32[]{:S(2)}) copy-start(f32[256,24]{0,1:T(8,128)} %copy.391) | copy-start | bytes 73732 | tf_op jit(solution)/shard_map/transpose(jvp())/while
  970.9 39.9 %copy-start.56 = (f32[24]{0:T(128)S(1)}, f32[24]{0:T(128)}, u32[]{:S(2)}) copy-start(f32[24]{0:T(128)} %get-tuple-element.1213) | copy-start | bytes 292 | tf_op jit(solution)/shard_map/transpose(jvp())/while
  971.0 40.5 %copy-start.15 = (f32[4,1,256,128]{3,2,1,0:T(8,128)S(1)}, f32[4,1,256,128]{3,2,1,0:T(8,128)}, u32[]{:S(2)}) copy-start(f32[4,1,256,128]{3,2,1,0:T(8,128)} %copy-done.14) | copy-start | bytes 1572868 | tf_op jit(solution)/shard_map/transpose(jvp())/while
  971.0 40.5 %copy-start.41 = (f32[24]{0:T(128)S(1)}, f32[24]{0:T(128)}, u32[]{:S(2)}) copy-start(f32[24]{0:T(128)} %copy-done.40) | copy-start | bytes 292 | tf_op jit(solution)/shard_map/transpose(jvp())/while
  1028.4 19.7 copy-start.25
  1028.4 19.7 copy-start.27
  1028.4 19.7 copy-start.29
  1028.4 19.7 copy-start.31
  1060.0 15.1 copy-start.9
  1060.0 15.1 copy-start.50
  1060.0 15.1 copy-start.52
  1060.0 15.1 copy-start.60
  1128.2 91.9 %copy-start.58 = (f32[24]{0:T(128)S(1)}, f32[24]{0:T(128)}, u32[]{:S(2)}) copy-start(f32[24]{0:T(128)} %get-tuple-element.474) | copy-start | bytes 292
  1128.2 95.3 %copy-start.61 = (f32[1536]{0:T(1024)S(1)}, f32[1536]{0:T(1024)}, u32[]{:S(2)}) copy-start(f32[1536]{0:T(1024)} %get-tuple-element.783) | copy-start | bytes 18436
  1267.1 265.1 %copy-start.64 = (f32[2]{0:T(128)S(1)}, f32[2]{0:T(128)}, u32[]{:S(2)}) copy-start(f32[2]{0:T(128)} %param.24) | copy-start | bytes 28
  1267.1 838.6 %all-gather.9.cloned.1.call-start = ((), (), s32[]{:S(2)}) async-start(), calls=%async_computation.5 | async-start | bytes 33914880 | tf_op jit(solution)/shard_map/all_gather | solution.py:25
  1531.4 863.5 %all-gather.7.cloned.1.call-start = ((), (), s32[]{:S(2)}) async-start(), calls=%async_computation.4 | async-start | bytes 18841600 | tf_op jit(solution)/shard_map/all_gather | solution.py:302
  2229.0 75.9 %all-to-all-start.1 = ((bf16[2,1024,768]{2,0,1:T(2,128)(2,1)}), bf16[2,1024,768]{2,0,1:T(2,128)(2,1)}, u32[]{:S(2)}, u32[]{:S(2)}) async-start(bf16[2,1024,768]{2,0,1:T(2,128)(2,1)} %copy.241), calls=%async_computation.1 | async-start | bytes 6291456 | tf_op jit(solution)/shard_map/all_to_all | solution.py:276
  2233.8 74.7 %copy-start.55 = (s32[8,2]{1,0:T(8,128)S(1)}, s32[8,2]{1,0:T(8,128)}, u32[]{:S(2)}) copy-start(s32[8,2]{1,0:T(8,128)} %get-tuple-element.789) | copy-start | bytes 196
  2304.8 74.5 %all-to-all-start.2 = ((bf16[2,1024,768]{2,0,1:T(2,128)(2,1)}), bf16[2,1024,768]{2,0,1:T(2,128)(2,1)S(1)}, u32[]{:S(2)}, u32[]{:S(2)}) async-start(bf16[2,1024,768]{2,0,1:T(2,128)(2,1)} %copy.255), calls=%async_computation.2 | async-start | bytes 6291456 | tf_op jit(solution)/shard_map/all_to_all | solution.py:277
  (59 other events, 461.1 us)
Sparse Core Ops, SparseCore 0:
  11.0 56.1 all-gather.4
  1267.2 259.9 all-reduce.22
  1531.5 574.0 all-gather.8
  2186.7 96.2 all-gather.6
